TPU v7x, 128 devices: a whole 4x4x4 slice. The times are simulated.
128 devices in a mesh: lat: 8 (over y_lo, x), lon: 16 (over z, y_hi, core).
Axes of the slice: x: 4, y: 4 (y_hi: 2, y_lo: 2; y = y_hi * 2 + y_lo), z: 4, core: 2. Of those that a mesh axis runs over, the one named last changes fastest.
Arguments:
- grad_out: bfloat16 [1, 720, 128, 1440], P(None, 'lat', None, 'lon'), may hold values from -6 to 6
- spectrum: bfloat16 [640, 720, 1, 2, 128], P('lon', 'lat'), may hold values from -0.8984375 to 0.8984375
- weights: bfloat16 [720, 128, 128], P('lat'), may hold values from -0.5 to 0.5
Outputs:
- grad_in: bfloat16 [1, 720, 128, 1440], P(None, 'lat', None, 'lon')
- weight_grad: float32 [720, 128, 128], P('lat', 'lon')
All inputs are finite; a program needn't handle non-finite values.
Results may differ from a plain program's by a relative error of at most 0.015.
Values may be sent and summed in bfloat16 or wider, within the bound.
No kernel may reach another device: no remote copies, remote signals or barrier semaphores. Data moves between devices by JAX's collectives and lax.ppermute only.
A program may use at most 128 MiB of HBM per device.

v0:
```python
import math

import jax
import jax.numpy as jnp
import numpy as np
from jax import lax
from jax.experimental import pallas as pl
from jax.experimental.pallas import tpu as pltpu
from jax.sharding import PartitionSpec as P

LAT = 720
LON = 1440
L = 720
M = 640
C = 128
LATS = 8
LONS = 16
DEVICES = LATS * LONS
ROWS = LAT // LATS
COLS = LON // LONS
SLOT = 6
USED = ROWS // SLOT
PAD = 96
ODD = PAD + 1
ORDERS = M // (LATS * LONS)
HALF = LONS // 2
Q = 2 * ORDERS
CHUNK = Q * SLOT
DEGREES = L // LATS
BLOCK = 16
TAIL = 4
SHIFT = 40

F32 = jnp.float32
BF16 = jnp.bfloat16


def limit(mebibytes):
    return pltpu.CompilerParams(vmem_limit_bytes=mebibytes << 20)


def near(x):
    return pltpu.with_memory_space_constraint(x, pltpu.VMEM)


def far(x):
    return pltpu.with_memory_space_constraint(x, pltpu.HBM)


def whole(space=pltpu.VMEM):
    return pl.BlockSpec(memory_space=space)


def stream(table, held, ready, steps):
    g = pl.program_id(0)

    def copy(step):
        return pltpu.make_async_copy(table.at[step], held.at[step], ready.at[step])

    @pl.when(g == 0)
    def _():
        for step in range(steps):
            copy(step).start()

    def arrive():
        @pl.when(g < steps)
        def _():
            copy(jnp.minimum(g, steps - 1)).wait()

    return arrive


def fetch(table, held, ready):
    parts = range(held.shape[0])
    copies = [pltpu.make_async_copy(table.at[k], held.at[k], ready.at[k]) for k in parts]
    for copy in copies:
        copy.start()
    return copies


def send(made, out, done):
    copy = pltpu.make_async_copy(made, out, done)
    copy.start()
    return copy


def finish(copies):
    for copy in copies:
        copy.wait()


def streamed(table):
    return [pltpu.VMEM(table.shape, table.dtype), pltpu.SemaphoreType.DMA((table.shape[0],))]


def cosine_values(position, order, part):
    step = position * order + part * (LON // 4)
    turn = step - LON * jnp.floor(step * (1.0 / LON))
    fold = (LON // 4) - jnp.abs(turn - LON // 2)
    angle = fold * (2.0 * math.pi / LON)
    square = angle * angle
    series = -1.0 / 39916800.0
    for term in (1.0 / 362880.0, -1.0 / 5040.0, 1.0 / 120.0, -1.0 / 6.0, 1.0):
        series = series * square + term
    return -(angle * series) * (1.0 / math.sqrt(LON))


def fourier_tables():
    def line(shape, axis):
        at = lax.broadcasted_iota(jnp.int32, shape, axis)
        inner = at % PAD
        return (at // PAD * COLS + inner).astype(F32), (inner < COLS).astype(F32)

    def modes(shape, axis):
        at = lax.broadcasted_iota(jnp.int32, shape, axis)
        device, kind = at // Q, at % Q
        parity, device = device // (DEVICES // 2), device % (DEVICES // 2)
        lat = device // LONS * 2 + parity
        order = device % LONS * (LATS * ORDERS) + kind // 2 * LATS + lat
        return order.astype(F32), (kind % 2).astype(F32)

    wide = HALF * PAD
    position, live = line((1, wide), 1)
    order, part = modes((2 * M, 1), 0)
    forward = (cosine_values(position, order, part) * live).astype(BF16)
    position, live = line((wide, 1), 0)
    order, part = modes((1, 2 * M), 1)
    backward = (cosine_values(position, order, part) * live).astype(BF16)
    return forward.reshape(2, M, wide), backward


def seed_constants():
    out = []
    for m in range(M):
        out.append(
            0.5 * math.log(m + 0.5)
            + 0.5 * math.lgamma(2.0 * m + 1.0)
            - math.lgamma(m + 1.0)
            - m * math.log(2.0)
        )
    return np.asarray(out, np.float32)


def legendre_kernel(up, back, start, seed, order, x_ref, root_ref, sine_ref, out, buf):
    x = x_ref[...]
    root = root_ref[...]
    base = [seed[k] + order[k] * sine_ref[...] for k in range(ORDERS)]
    zero = jnp.zeros_like(x)
    small = 2.0**-SHIFT
    unit = SHIFT * math.log(2.0)

    def block(first, row, steps, carry):
        current, previous, count = (list(part) for part in carry)
        factor = [None] * ORDERS
        for offset in range(steps):
            if offset % 8 == 0:
                for k in range(ORDERS):
                    big = jnp.maximum(jnp.abs(current[k]), jnp.abs(previous[k])) > 1.0
                    scale = jnp.where(big, small, 1.0)
                    current[k] = current[k] * scale
                    previous[k] = previous[k] * scale
                    count[k] = count[k] + jnp.where(big, 1.0, 0.0)
                    factor[k] = jnp.exp(base[k] + unit * count[k]) * root
            for k in range(ORDERS):
                at = k * L + first + offset
                advanced = (up[at] * x) * current[k] - back[at] * previous[k] + start[at]
                previous[k] = current[k]
                current[k] = advanced
                buf[k, offset * 8 : offset * 8 + 8, :] = advanced * factor[k]
        for k in range(ORDERS):
            for offset in range(steps, BLOCK):
                buf[k, offset * 8 : offset * 8 + 8, :] = zero
            for tt in range(SLOT):
                low = buf[k, pl.ds(tt, 8, stride=8), :]
                high = buf[k, pl.ds(64 + tt, 8, stride=8), :]
                both = jnp.concatenate([low, high], axis=0).astype(BF16)
                out[k, pl.ds(pl.multiple_of(row, BLOCK), BLOCK), tt * 128 : tt * 128 + 128] = both
        return tuple(current), tuple(previous), tuple(count)

    def band(k, carry):
        first, row = k * DEGREES, k * PAD
        whole = DEGREES // BLOCK

        def inner(step, carry):
            return block(first + step * BLOCK, row + step * BLOCK, BLOCK, carry)

        carry = lax.fori_loop(0, whole, inner, carry)
        done = whole * BLOCK
        return block(first + done, row + done, DEGREES - done, carry)

    none = (zero,) * ORDERS
    lax.fori_loop(0, LATS, band, (none, none, none))


def legendre_table():
    lon, lat = lax.axis_index("lon"), lax.axis_index("lat")
    orders = (lon * ORDERS + jnp.arange(ORDERS, dtype=jnp.int32)) * LATS + lat
    order = orders.astype(F32)
    seeds = jnp.asarray(seed_constants().reshape(LONS, ORDERS, LATS))
    seed = lax.dynamic_slice(seeds, (lon, 0, lat), (1, ORDERS, 1)).reshape(ORDERS)
    slot = jnp.arange(1024, dtype=jnp.int32)
    tt, device = slot // DEVICES, slot % DEVICES
    lat, lon = device // LONS, device % LONS
    live = (tt < SLOT) & (lon < USED)
    row = jnp.where(live, ROWS * lat + SLOT * lon + tt, 0)
    angle = (row.astype(F32) + 0.5) * (math.pi / LAT)
    sine = jnp.sin(angle)
    x = jnp.where(live, jnp.cos(angle), 0.0).reshape(8, 128)
    root = jnp.where(live, jnp.sqrt(sine * (math.pi / LAT)), 0.0).reshape(8, 128)
    log_sine = jnp.log(sine).reshape(8, 128)
    degree = jnp.arange(L, dtype=jnp.int32)[None, :]
    past = degree > orders[:, None]
    val, ord_val = degree.astype(F32), order[:, None]
    divisor = jnp.where(past, val * val - ord_val * ord_val, 1.0)
    up = jnp.where(past, jnp.sqrt(jnp.maximum((4.0 * val * val - 1.0) / divisor, 0.0)), 0.0)
    lower = (val - 1.0) * (val - 1.0) - ord_val * ord_val
    back = jnp.sqrt(
        jnp.maximum(lower * (2.0 * val + 1.0) / ((2.0 * val - 3.0) * divisor), 0.0)
    )
    back = jnp.where(past, back, 0.0)
    start = (degree == orders[:, None]).astype(F32)
    smem = pl.BlockSpec(memory_space=pltpu.SMEM)
    vmem = pl.BlockSpec(memory_space=pltpu.VMEM)
    return pl.pallas_call(
        legendre_kernel,
        out_shape=jax.ShapeDtypeStruct((ORDERS, LATS * PAD, DEVICES * SLOT), BF16),
        in_specs=[smem] * 5 + [vmem] * 3,
        out_specs=vmem,
        scratch_shapes=[pltpu.VMEM((ORDERS, 8 * BLOCK, 128), F32)],
        compiler_params=limit(16),
        name="legendre",
    )(up.reshape(-1), back.reshape(-1), start.reshape(-1), seed, order, x, root, log_sine)


def forward_kernel(table, x_ref, out_ref, buf, held, ready):
    g = pl.program_id(0)
    arrive = stream(table, held, ready, 2)
    arrive()
    rows = LONS * Q

    for parity in range(2):

        @pl.when(g == parity)
        def _():
            for pair in range(SLOT // 2):
                both = []
                for half in range(2):
                    low = x_ref[:HALF, 2 * pair + half]
                    high = x_ref[HALF:, 2 * pair + half]
                    both.append((low - high if parity else low + high).reshape(HALF * PAD, C))
                done = jnp.dot(
                    held[parity], jnp.concatenate(both, axis=1), preferred_element_type=F32
                )
                for half in range(2):
                    for lat in range(LATS // 2):
                        first = lat * rows * SLOT + 2 * pair + half
                        buf[pl.ds(first, rows, stride=SLOT), :] = done[
                            lat * rows : lat * rows + rows, half * C : half * C + C
                        ]

    for lat in range(LATS // 2):
        first = lat * rows * SLOT
        out_ref[lat, 0] = buf[first : first + rows * SLOT, :].astype(BF16)


def fourier_forward(table, x):
    shape = (LATS // 2, 2, LONS * CHUNK, C)
    return pl.pallas_call(
        forward_kernel,
        grid=(2,),
        out_shape=pltpu.HBM(shape, BF16),
        in_specs=[whole(pltpu.HBM), whole()],
        out_specs=pl.BlockSpec((shape[0], 1) + shape[2:], lambda g: (0, g, 0, 0)),
        scratch_shapes=[pltpu.VMEM((M * SLOT, C), F32)] + streamed(table),
        compiler_params=limit(24),
        name="fourier_forward",
    )(far(table), near(x))


def analyse_kernel(table, x_ref, out_ref, wide, held, ready):
    g = pl.program_id(0)
    arrive = stream(table, held, ready, ORDERS)

    @pl.when(g == 0)
    def _():
        wide[...] = x_ref[...].astype(F32)

    def column(q):
        parts = [wide[pl.ds(q * SLOT + tt, DEVICES, stride=CHUNK), :] for tt in range(SLOT)]
        return jnp.concatenate(parts, axis=0).astype(BF16)

    right = jnp.concatenate([column(2 * g), column(2 * g + 1)], axis=1)
    arrive()
    done = jnp.dot(held[g], right, preferred_element_type=F32).astype(BF16)
    for half in range(2):
        out_ref[:, half] = done[:, half * C : half * C + C].reshape(LATS, PAD, C)


def analyse(table, x):
    return pl.pallas_call(
        analyse_kernel,
        grid=(ORDERS,),
        out_shape=pltpu.HBM((LATS, Q, PAD, C), BF16),
        in_specs=[whole(pltpu.HBM), whole()],
        out_specs=pl.BlockSpec((LATS, 2, PAD, C), lambda g: (0, g, 0, 0)),
        scratch_shapes=[pltpu.VMEM((DEVICES * CHUNK, C), F32)] + streamed(table),
        compiler_params=limit(26),
        name="analyse",
    )(far(table), near(x))


def mix_kernel(x_ref, weights, gathered, out_ref, wide, mixed, rows, made, held, ready, done):
    copies = fetch(weights, held, ready)
    steps, each = held.shape[:2]
    slabs = LATS * Q
    for slab in range(slabs):
        wide[slab * ODD : slab * ODD + PAD, :] = x_ref[slab * PAD : slab * PAD + PAD, :].astype(
            F32
        )
        mixed[slab * ODD + PAD - 8 : slab * ODD + PAD, :] = jnp.zeros((8, C), F32)
    sent = []
    for step in range(steps):
        copies[step].wait()
        for offset in range(each):
            degree = step * each + offset
            across = pl.ds(degree, slabs, stride=ODD)
            part = wide[across, :].astype(BF16)
            rows[degree] = part
            mixed[across, :] = lax.dot_general(
                part, held[step, offset], (((1,), (1,)), ((), ())), preferred_element_type=F32
            )
        block = pl.ds(step * each, each)
        sent.append(send(rows.at[block], gathered.at[block], done.at[step]))
    for step in range(TAIL):
        first = step * (slabs // TAIL)
        for slab in range(first, first + slabs // TAIL):
            made[slab * PAD : slab * PAD + PAD, :] = mixed[
                slab * ODD : slab * ODD + PAD, :
            ].astype(BF16)
        block = pl.ds(first * PAD, slabs // TAIL * PAD)
        sent.append(send(made.at[block], out_ref.at[block], done.at[steps + step]))
    finish(sent)


def mix(x, weights):
    steps = 5
    size = LATS * Q * PAD
    weights = weights.reshape(steps, DEGREES // steps, C, C)
    return pl.pallas_call(
        mix_kernel,
        out_shape=(
            pltpu.HBM((DEGREES, LATS * Q, C), BF16),
            pltpu.HBM((size, C), BF16),
        ),
        in_specs=[whole(), whole(pltpu.HBM)],
        out_specs=(whole(pltpu.HBM), whole(pltpu.HBM)),
        scratch_shapes=[pltpu.VMEM((LATS * Q * ODD, C), F32)] * 2
        + [pltpu.VMEM((DEGREES, LATS * Q, C), BF16), pltpu.VMEM((size, C), BF16)]
        + streamed(weights)
        + [pltpu.SemaphoreType.DMA((steps + TAIL,))],
        compiler_params=limit(28),
        name="mix",
    )(near(x), far(weights))


def weigh_kernel(place, stored, gathered, keep, give):
    core, z = place[0], place[1]
    share = C // LONS
    for offset in range(stored.shape[0]):
        part = lax.dot_general(
            stored[offset], gathered[offset], (((0,), (0,)), ((), ())), preferred_element_type=F32
        )
        for column in range(4):
            to = lax.rem(column + 4 - z, 4)
            piece = part[column * 4 * share : column * 4 * share + 4 * share]
            here = jnp.concatenate([piece[:share], piece[2 * share : 3 * share]], axis=0)
            there = jnp.concatenate([piece[share : 2 * share], piece[3 * share :]], axis=0)
            keep[to, offset] = jnp.where(core == 0, here, there).astype(BF16)
            give[to, offset] = jnp.where(core == 0, there, here).astype(BF16)


def weigh(stored, gathered):
    steps = 5
    each = DEGREES // steps
    lon = lax.axis_index("lon")
    shape = (4, DEGREES, C // 8, C)
    rows = pl.BlockSpec((each, LATS * Q, C), lambda g: (g, 0, 0))
    sums = pl.BlockSpec((4, each, C // 8, C), lambda g: (0, g, 0, 0))
    return pl.pallas_call(
        weigh_kernel,
        grid=(steps,),
        out_shape=(pltpu.HBM(shape, BF16), pltpu.HBM(shape, BF16)),
        in_specs=[pl.BlockSpec(memory_space=pltpu.SMEM), rows, rows],
        out_specs=(sums, sums),
        compiler_params=limit(20),
        name="weigh",
    )(jnp.stack([lon & 1, lon >> 2]), far(stored), far(gathered))


def synthesise_kernel(table, x_ref, out_ref, made, held, ready):
    g = pl.program_id(0)
    arrive = stream(table, held, ready, ORDERS)
    arrive()
    right = jnp.concatenate(
        [x_ref[:, 2 * g + half].reshape(LATS * PAD, C) for half in range(2)], axis=1
    )
    done = jnp.dot(held[g], right, preferred_element_type=F32)
    for half in range(2):
        for tt in range(SLOT):
            made[pl.ds((2 * g + half) * SLOT + tt, DEVICES, stride=CHUNK), :] = done[
                tt * DEVICES : tt * DEVICES + DEVICES, half * C : half * C + C
            ]

    @pl.when(g == ORDERS - 1)
    def _():
        out_ref[...] = made[...].astype(BF16)


def synthesise(table, x):
    return pl.pallas_call(
        synthesise_kernel,
        grid=(ORDERS,),
        out_shape=pltpu.HBM((DEVICES * CHUNK, C), BF16),
        in_specs=[whole(pltpu.HBM), whole()],
        out_specs=pl.BlockSpec((DEVICES * CHUNK, C), lambda g: (0, 0)),
        scratch_shapes=[pltpu.VMEM((DEVICES * CHUNK, C), F32)] + streamed(table),
        compiler_params=limit(26),
        name="synthesise",
    )(far(table), near(x))


def backward_kernel(table, x_ref, out_ref, wide, right, held, ready):
    g = pl.program_id(0)
    arrive = stream(table, held, ready, held.shape[0])
    rows = LONS * Q

    @pl.when(g == 0)
    def _():
        wide[...] = x_ref[...].astype(F32)
        for tt in range(SLOT):
            part = wide[pl.ds(tt, 2 * M, stride=SLOT), :].astype(BF16)
            for lat in range(LATS):
                first = lat // 2 * rows
                right[lat % 2, first : first + rows, tt * C : tt * C + C] = part[
                    lat * rows : lat * rows + rows
                ]

    arrive()
    for pair in range(SLOT // 2):
        lanes = slice(2 * pair * C, 2 * pair * C + 2 * C)
        even = jnp.dot(held[g, :, :M], right[0, :, lanes], preferred_element_type=F32)
        odd = jnp.dot(held[g, :, M:], right[1, :, lanes], preferred_element_type=F32)
        for side, done in enumerate((even + odd, even - odd)):
            done = done.astype(BF16)
            for half in range(2):
                for j in range(out_ref.shape[1]):
                    out_ref[side, j, 2 * pair + half] = done[
                        j * PAD : j * PAD + PAD, half * C : half * C + C
                    ]


def fourier_backward(table, x):
    steps = 2
    each = HALF // steps
    table = table.reshape(steps, each * PAD, 2 * M)
    return pl.pallas_call(
        backward_kernel,
        grid=(steps,),
        out_shape=pltpu.HBM((2, HALF, SLOT, PAD, C), BF16),
        in_specs=[whole(pltpu.HBM), whole()],
        out_specs=pl.BlockSpec((2, each, SLOT, PAD, C), lambda g: (0, g, 0, 0, 0)),
        scratch_shapes=[
            pltpu.VMEM((DEVICES * CHUNK, C), F32),
            pltpu.VMEM((2, M, SLOT * C), BF16),
        ]
        + streamed(table),
        compiler_params=limit(26),
        name="fourier_backward",
    )(far(table), near(x))


def exchange(x, axis):
    return lax.all_to_all(x, axis, split_axis=0, concat_axis=0, tiled=True)


def cells(x):
    return x.reshape(DEVICES, CHUNK // 2, 2, C)


def on_device(grad_out, spectrum, weights):
    both = ("lat", "lon")
    rows = jnp.swapaxes(grad_out[0], 1, 2)
    rows = jnp.pad(rows, ((0, LONS * SLOT - ROWS), (0, PAD - COLS), (0, 0)))
    rows = exchange(rows.reshape(LONS, SLOT, PAD, C), "lon")
    forward, backward = fourier_tables()
    legendre = legendre_table()
    rows, forward, legendre = lax.optimization_barrier((rows, forward, legendre))

    spectra = fourier_forward(forward, rows)
    columns = exchange(cells(spectra), both).reshape(DEVICES * CHUNK, C)
    turned = jnp.swapaxes(legendre, 1, 2)
    stored = spectrum.reshape(ORDERS, LATS, DEGREES, 2, C).transpose(2, 1, 0, 3, 4)
    stored = stored.reshape(DEGREES, LATS * Q, C)
    columns, turned, stored = lax.optimization_barrier((columns, turned, stored))

    analysed = exchange(analyse(legendre, columns), "lat").reshape(LATS * Q * PAD, C)
    analysed, backward = lax.optimization_barrier((analysed, backward))
    gathered, spec_local = mix(analysed, weights)
    spec_grad = exchange(spec_local.reshape(LATS, Q, PAD, C), "lat")

    keep, give = weigh(stored, gathered)
    got = lax.ppermute(give, "lon", [(k, k ^ 1) for k in range(LONS)])
    sums = [keep[step].astype(F32) + got[step].astype(F32) for step in range(4)]
    held, got = sums[0], []
    for step in (1, 3, 2):
        pairs = [(k, (k + 4 * step) % LONS) for k in range(LONS)]
        got.append(lax.ppermute(sums[step].astype(BF16), "lon", pairs))
    spec_grad, held = lax.optimization_barrier((spec_grad, held))

    row_block = synthesise(turned, spec_grad)
    row_block = exchange(cells(row_block), both)
    for part in got:
        held = held + part.astype(F32)
    held = held.reshape(DEGREES, 2, C // LONS, C)
    y = (lax.axis_index("lon") >> 1) & 1
    keep = lax.dynamic_index_in_dim(held, y, 1, keepdims=False)
    give = lax.dynamic_index_in_dim(held, 1 - y, 1, keepdims=False).astype(BF16)
    got = lax.ppermute(give, "lon", [(k, k ^ 2) for k in range(LONS)])
    weight_grad = keep + got.astype(F32)
    row_block, weight_grad = lax.optimization_barrier((row_block, weight_grad))
    grid_part = fourier_backward(backward, row_block.reshape(DEVICES * CHUNK, C))
    grid_part = exchange(grid_part.reshape(LONS, SLOT, PAD, C), "lon")
    grad_in = grid_part[:USED].reshape(ROWS, PAD, C)[:, :COLS]
    return jnp.swapaxes(grad_in, 1, 2)[None], weight_grad


def solution(mesh):
    in_specs = (
        P(None, "lat", None, "lon"),
        P("lon", "lat", None, None, None),
        P("lat", None, None),
    )
    out_specs = (P(None, "lat", None, "lon"), P("lat", "lon", None))
    return jax.shard_map(
        on_device, mesh=mesh, in_specs=in_specs, out_specs=out_specs, check_vma=False
    )
```

profile of v0, /device:TPU:0, one launch (start us, length us, event | category | flops | bytes accessed | tf_op | source)
XLA Modules:
  0.0 271.8 jit_solution(13774492801138804654)
XLA Ops:
  0.6 3.3 %pad.4 = bf16[96,96,128]{2,1,0:T(8,128)(2,1)} pad(bf16[90,90,128]{2,1,0:T(8,128)(2,1)} %bitcast.57, bf16[]{:T(256)} %constant.277.clone.1), padding=0_6x0_6x0_0 | pad | bytes 4432898 | tf_op jit(solution)/shard_map/jit(_pad)/pad | solution.py:493
  3.9 8.2 %all-to-all-start = ((bf16[16,6,96,128]{3,2,1,0:T(8,128)(2,1)}), bf16[16,6,96,128]{3,2,1,0:T(8,128)(2,1)S(1)}, u32[]{:S(2)}, u32[]{:S(2)}) async-start(bf16[16,6,96,128]{3,2,1,0:T(8,128)(2,1)} %bitcast.50), calls=%async_computation | async-start | bytes 4718592 | tf_op jit(solution)/shard_map/all_to_all | solution.py:483
  12.1 0.1 subtract_multiply_fusion
  12.2 0.1 mul.419
  12.3 0.1 sub.152
  12.3 0.1 fusion.10
  12.4 0.1 gt.23
  12.6 0.1 div.175
  12.6 0.1 mul.421
  12.7 0.1 reshape.688.start
  12.8 0.7 fusion.76.seed
  13.5 0.1 fusion.75.sine_ref
  13.6 0.1 sqrt_select_fusion.2
  13.7 9.1 %legendre.1.table = bf16[5,768,768]{2,1,0:T(8,128)(2,1)S(1)} custom-call(f32[3600]{0:T(1024)S(1)} %get-tuple-element.41.up, f32[3600]{0:T(1024)S(1)} %get-tuple-element.40.back, f32[3600]{0:T(1024)S(1)} %reshape.688.start, f32[5]{0:T(128)S(1)} %fusion.76.seed, f32[5]{0:T(128)S(1)} %get-tuple-element.34.order, f32[8,128]{1,0:T(8,128)S(1)} %get-tuple-element.49.x_ref, ...), custom_call_target="tpu_custom_call" | custom-call | tf_op jit(solution)/shard_map/legendre/pallas_call | solution.py:224
  22.8 0.0 copy-start
  22.8 2.5 copy-done
  25.4 0.1 fusion.48
  25.5 4.3 %multiply_convert_fusion.1.table = bf16[2,640,768]{2,1,0:T(8,128)(2,1)} fusion(f32[768]{0:T(1024)S(1)} %fusion.69, f32[2,640]{1,0:T(2,128)S(1)} %fusion.46, f32[2,640]{1,0:T(2,128)S(1)} %fusion.48, f32[768]{0:T(1024)S(1)} %fusion.54), kind=kLoop, calls=%fused_computation.7 | loop fusion | flops 24576000 | bytes 1982464 | tf_op jit(solution)/shard_map/convert_element_type | solution.py:125
  29.8 14.3 %all-to-all-done.x_ref = bf16[16,6,96,128]{3,2,1,0:T(8,128)(2,1)S(1)} async-done(((bf16[16,6,96,128]{3,2,1,0:T(8,128)(2,1)}), bf16[16,6,96,128]{3,2,1,0:T(8,128)(2,1)S(1)}, u32[]{:S(2)}, u32[]{:S(2)}) %all-to-all-start) | async-done | bytes 2359328 | tf_op jit(solution)/shard_map/all_to_all | solution.py:483
  44.1 4.3 %fourier_forward.1 = bf16[4,2,960,128]{3,2,1,0:T(8,128)(2,1)} custom-call(bf16[2,640,768]{2,1,0:T(8,128)(2,1)} %multiply_convert_fusion.1.table, bf16[16,6,96,128]{3,2,1,0:T(8,128)(2,1)S(1)} %all-to-all-done.x_ref), custom_call_target="tpu_custom_call" | custom-call | tf_op jit(solution)/shard_map/fourier_forward/pallas_call | solution.py:268
  48.5 6.2 %all-to-all-start.1 = ((bf16[128,30,2,128]{3,2,1,0:T(2,128)(2,1)}), bf16[128,30,2,128]{3,2,1,0:T(2,128)(2,1)S(1)}, u32[]{:S(2)}, u32[]{:S(2)}) async-start(bf16[128,30,2,128]{3,2,1,0:T(2,128)(2,1)} %bitcast.54), calls=%async_computation.1 | async-start | bytes 3932160 | tf_op jit(solution)/shard_map/all_to_all | solution.py:483
  54.7 4.0 %copy.7 = bf16[5,8,90,2,128]{4,3,0,1,2:T(2,128)(2,1)} copy(bf16[5,8,90,2,128]{4,3,2,1,0:T(2,128)(2,1)} %bitcast.59) | data formatting | bytes 3686400 | tf_op jit(solution)/shard_map/reshape | solution.py:502
  58.7 9.1 %copy.6 = bf16[5,768,768]{1,2,0:T(8,128)(2,1)} copy(bf16[5,768,768]{2,1,0:T(8,128)(2,1)} %copy-done) | data formatting | bytes 11796480 | tf_op jit(solution)/shard_map/optimization_barrier | solution.py:497
  67.8 14.4 %all-to-all-done.1 = bf16[128,30,2,128]{3,2,1,0:T(2,128)(2,1)S(1)} async-done(((bf16[128,30,2,128]{3,2,1,0:T(2,128)(2,1)}), bf16[128,30,2,128]{3,2,1,0:T(2,128)(2,1)S(1)}, u32[]{:S(2)}, u32[]{:S(2)}) %all-to-all-start.1) | async-done | bytes 1966112 | tf_op jit(solution)/shard_map/all_to_all | solution.py:483
  82.1 5.1 %analyse.1 = bf16[8,10,96,128]{3,2,1,0:T(8,128)(2,1)} custom-call(bf16[5,768,768]{2,1,0:T(8,128)(2,1)} %copy-done, bf16[7680,128]{1,0:T(8,128)(2,1)S(1)} %bitcast.45), custom_call_target="tpu_custom_call" | custom-call | tf_op jit(solution)/shard_map/analyse/pallas_call | solution.py:300
  87.3 3.8 %all-to-all-start.2 = ((bf16[8,10,96,128]{3,2,1,0:T(8,128)(2,1)}), bf16[8,10,96,128]{3,2,1,0:T(8,128)(2,1)S(1)}, u32[]{:S(2)}, u32[]{:S(2)}) async-start(bf16[8,10,96,128]{3,2,1,0:T(8,128)(2,1)} %analyse.1), calls=%async_computation.2 | async-start | bytes 3932160 | tf_op jit(solution)/shard_map/all_to_all | solution.py:483
  91.1 0.1 pad_add_fusion.place
  91.2 4.6 %multiply_convert_fusion = bf16[768,1280]{1,0:T(8,128)(2,1)} fusion(f32[768]{0:T(1024)S(1)} %fusion.69, f32[1280]{0:T(1024)S(1)} %fusion.25, f32[1280]{0:T(1024)S(1)} %fusion.20, f32[768]{0:T(1024)S(1)} %fusion.54), kind=kLoop, calls=%fused_computation | loop fusion | flops 24576000 | bytes 1982464 | tf_op jit(solution)/shard_map/convert_element_type | solution.py:128
  95.8 21.8 %all-to-all-done.2 = bf16[8,10,96,128]{3,2,1,0:T(8,128)(2,1)S(1)} async-done(((bf16[8,10,96,128]{3,2,1,0:T(8,128)(2,1)}), bf16[8,10,96,128]{3,2,1,0:T(8,128)(2,1)S(1)}, u32[]{:S(2)}, u32[]{:S(2)}) %all-to-all-start.2) | async-done | bytes 1966112 | tf_op jit(solution)/shard_map/all_to_all | solution.py:483
  117.6 5.2 %mix.1 = (bf16[90,80,128]{2,1,0:T(8,128)(2,1)}, bf16[7680,128]{1,0:T(8,128)(2,1)}) custom-call(bf16[7680,128]{1,0:T(8,128)(2,1)S(1)} %bitcast.47, bf16[5,18,128,128]{3,2,1,0:T(8,128)(2,1)} %bitcast.56), custom_call_target="tpu_custom_call" | custom-call | tf_op jit(solution)/shard_map/mix/pallas_call | solution.py:349
  122.8 5.9 %weigh.1 = (bf16[4,90,16,128]{3,2,1,0:T(8,128)(2,1)}, bf16[4,90,16,128]{3,2,1,0:T(8,128)(2,1)}) custom-call(s32[2]{0:T(128)S(1)} %pad_add_fusion.place, bf16[90,80,128]{2,1,0:T(8,128)(2,1)} %bitcast.55, bf16[90,80,128]{2,1,0:T(8,128)(2,1)} %get-tuple-element.27.gathered), custom_call_target="tpu_custom_call" | custom-call | tf_op jit(solution)/shard_map/weigh/pallas_call | solution.py:389
  128.7 0.0 collective-permute-start
  128.7 8.5 %all-to-all-start.3 = ((bf16[8,10,96,128]{3,2,1,0:T(8,128)(2,1)}), bf16[8,10,96,128]{3,2,1,0:T(8,128)(2,1)S(1)}, u32[]{:S(2)}, u32[]{:S(2)}) async-start(bf16[8,10,96,128]{3,2,1,0:T(8,128)(2,1)} %bitcast.58), calls=%async_computation.3 | async-start | bytes 3932160 | tf_op jit(solution)/shard_map/all_to_all | solution.py:483
  137.2 0.0 collective-permute-done
  137.2 0.0 copy-start.1
  137.2 1.2 copy-done.1
  138.4 3.0 %fusion.6 = (bf16[90,16,128]{2,1,0:T(8,128)(2,1)}, bf16[90,16,128]{2,1,0:T(8,128)(2,1)}, bf16[90,16,128]{2,1,0:T(8,128)(2,1)}, f32[90,16,128]{2,1,0:T(8,128)S(1)}) fusion(bf16[4,90,16,128]{3,2,1,0:T(8,128)(2,1)} %copy-done.1, bf16[4,90,16,128]{3,2,1,0:T(8,128)(2,1)} %get-tuple-element.28), kind=kLoop, calls=%fused_computation.20 | loop fusion | flops 2764800 | bytes 4792320 | tf_op jit(solution)/shard_map/convert_element_type | solution.py:517
  141.4 22.0 %all-to-all-done.3.x_ref = bf16[8,10,96,128]{3,2,1,0:T(8,128)(2,1)S(1)} async-done(((bf16[8,10,96,128]{3,2,1,0:T(8,128)(2,1)}), bf16[8,10,96,128]{3,2,1,0:T(8,128)(2,1)S(1)}, u32[]{:S(2)}, u32[]{:S(2)}) %all-to-all-start.3) | async-done | bytes 1966112 | tf_op jit(solution)/shard_map/all_to_all | solution.py:483
  163.4 5.3 %synthesise.1 = bf16[7680,128]{1,0:T(8,128)(2,1)} custom-call(bf16[5,768,768]{2,1,0:T(8,128)(2,1)} %bitcast.48, bf16[8,10,96,128]{3,2,1,0:T(8,128)(2,1)S(1)} %all-to-all-done.3.x_ref), custom_call_target="tpu_custom_call" | custom-call | tf_op jit(solution)/shard_map/synthesise/pallas_call | solution.py:420
  168.7 8.4 %all-to-all-start.4 = ((bf16[128,30,2,128]{3,2,1,0:T(2,128)(2,1)}), bf16[128,30,2,128]{3,2,1,0:T(2,128)(2,1)S(1)}, u32[]{:S(2)}, u32[]{:S(2)}) async-start(bf16[128,30,2,128]{3,2,1,0:T(2,128)(2,1)} %bitcast.52), calls=%async_computation.4 | async-start | bytes 3932160 | tf_op jit(solution)/shard_map/all_to_all | solution.py:483
  177.0 1.1 collective-permute-start.1
  178.2 2.2 collective-permute-start.2
  180.3 1.6 collective-permute-start.3
  182.0 27.8 %collective-permute-done.1 = bf16[90,16,128]{2,1,0:T(8,128)(2,1)S(1)} collective-permute-done((bf16[90,16,128]{2,1,0:T(8,128)(2,1)}, bf16[90,16,128]{2,1,0:T(8,128)(2,1)S(1)}, u32[]{:S(2)}, u32[]{:S(2)}) %collective-permute-start.1) | collective-permute-done | bytes 368672 | tf_op jit(solution)/shard_map/ppermute | solution.py:517
  209.8 0.0 copy-start.2
  209.8 0.0 collective-permute-done.2
  209.8 0.8 copy-done.2
  210.5 0.0 copy-start.3
  210.5 0.7 copy-done.3
  211.3 6.1 %collective-permute-done.3 = bf16[90,16,128]{2,1,0:T(8,128)(2,1)} collective-permute-done((bf16[90,16,128]{2,1,0:T(8,128)(2,1)}, bf16[90,16,128]{2,1,0:T(8,128)(2,1)}, u32[]{:S(2)}, u32[]{:S(2)}) %collective-permute-start.3) | collective-permute-done | bytes 368672 | tf_op jit(solution)/shard_map/ppermute | solution.py:517
  217.4 1.4 add_bitcast_fusion
  218.8 4.7 %collective-permute-start.4 = (bf16[90,8,128]{2,1,0:T(8,128)(2,1)S(1)}, bf16[90,8,128]{2,1,0:T(8,128)(2,1)S(1)}, u32[]{:S(2)}, u32[]{:S(2)}) collective-permute-start(bf16[90,8,128]{2,1,0:T(8,128)(2,1)S(1)} %fusion.9), channel_id=1, source_target_pairs={{0,2},{1,3},{2,0},{3,1},{4,6},{5,7},{6,4},{7,5},{8,10},{9,11},{10,... | collective-permute-start | bytes 552968 | tf_op jit(solution)/shard_map/ppermute | solution.py:528
  223.5 4.8 %collective-permute-done.4 = bf16[90,8,128]{2,1,0:T(8,128)(2,1)S(1)} collective-permute-done((bf16[90,8,128]{2,1,0:T(8,128)(2,1)S(1)}, bf16[90,8,128]{2,1,0:T(8,128)(2,1)S(1)}, u32[]{:S(2)}, u32[]{:S(2)}) %collective-permute-start.4) | collective-permute-done | bytes 184352 | tf_op jit(solution)/shard_map/ppermute | solution.py:528
  228.3 0.8 bitcast_add_fusion
  229.0 0.0 all-to-all-done.4
  229.0 4.4 %fourier_backward.1 = bf16[2,8,6,96,128]{4,3,2,1,0:T(8,128)(2,1)} custom-call(bf16[2,384,1280]{2,1,0:T(8,128)(2,1)} %bitcast.53, bf16[7680,128]{1,0:T(8,128)(2,1)S(1)} %bitcast.46), custom_call_target="tpu_custom_call" | custom-call | tf_op jit(solution)/shard_map/fourier_backward/pallas_call | solution.py:466
  233.5 36.6 %all_to_all.30 = bf16[16,6,96,128]{3,2,1,0:T(8,128)(2,1)S(1)} all-to-all(bf16[16,6,96,128]{3,2,1,0:T(8,128)(2,1)} %bitcast.49), channel_id=1, replica_groups=mesh['lat'=8,'lon'=16] {'lon'}, dimensions={0} | all-to-all | bytes 4718592 | tf_op jit(solution)/shard_map/all_to_all | solution.py:483
  270.1 0.1 slice.44
  270.3 1.5 slice_bitcast_fusion
  (15 shorter events, 0.2 us)
Async XLA Ops:
  3.9 40.2 %all-to-all-start = ((bf16[16,6,96,128]{3,2,1,0:T(8,128)(2,1)}), bf16[16,6,96,128]{3,2,1,0:T(8,128)(2,1)S(1)}, u32[]{:S(2)}, u32[]{:S(2)}) async-start(bf16[16,6,96,128]{3,2,1,0:T(8,128)(2,1)} %bitcast.50), calls=%async_computation | async-start | bytes 4718592 | tf_op jit(solution)/shard_map/all_to_all | solution.py:483
  22.8 2.5 copy-start
  48.5 33.7 %all-to-all-start.1 = ((bf16[128,30,2,128]{3,2,1,0:T(2,128)(2,1)}), bf16[128,30,2,128]{3,2,1,0:T(2,128)(2,1)S(1)}, u32[]{:S(2)}, u32[]{:S(2)}) async-start(bf16[128,30,2,128]{3,2,1,0:T(2,128)(2,1)} %bitcast.54), calls=%async_computation.1 | async-start | bytes 3932160 | tf_op jit(solution)/shard_map/all_to_all | solution.py:483
  87.3 30.3 %all-to-all-start.2 = ((bf16[8,10,96,128]{3,2,1,0:T(8,128)(2,1)}), bf16[8,10,96,128]{3,2,1,0:T(8,128)(2,1)S(1)}, u32[]{:S(2)}, u32[]{:S(2)}) async-start(bf16[8,10,96,128]{3,2,1,0:T(8,128)(2,1)} %analyse.1), calls=%async_computation.2 | async-start | bytes 3932160 | tf_op jit(solution)/shard_map/all_to_all | solution.py:483
  128.7 8.5 %collective-permute-start = (bf16[4,90,16,128]{3,2,1,0:T(8,128)(2,1)}, bf16[4,90,16,128]{3,2,1,0:T(8,128)(2,1)S(1)}, u32[]{:S(2)}, u32[]{:S(2)}) collective-permute-start(bf16[4,90,16,128]{3,2,1,0:T(8,128)(2,1)} %get-tuple-element.29), channel_id=1, source_target_pairs={{0,1},{1,0},{2,3},{3,2},{4,5},{5,4},{6,7},{7,6},{8,9},{9,8},{10,11... | collective-permute-start | bytes 4423688 | tf_op jit(solution)/shard_map/ppermute | solution.py:512
  128.7 34.7 %all-to-all-start.3 = ((bf16[8,10,96,128]{3,2,1,0:T(8,128)(2,1)}), bf16[8,10,96,128]{3,2,1,0:T(8,128)(2,1)S(1)}, u32[]{:S(2)}, u32[]{:S(2)}) async-start(bf16[8,10,96,128]{3,2,1,0:T(8,128)(2,1)} %bitcast.58), calls=%async_computation.3 | async-start | bytes 3932160 | tf_op jit(solution)/shard_map/all_to_all | solution.py:483
  137.2 1.2 copy-start.1
  168.7 60.4 %all-to-all-start.4 = ((bf16[128,30,2,128]{3,2,1,0:T(2,128)(2,1)}), bf16[128,30,2,128]{3,2,1,0:T(2,128)(2,1)S(1)}, u32[]{:S(2)}, u32[]{:S(2)}) async-start(bf16[128,30,2,128]{3,2,1,0:T(2,128)(2,1)} %bitcast.52), calls=%async_computation.4 | async-start | bytes 3932160 | tf_op jit(solution)/shard_map/all_to_all | solution.py:483
  177.0 32.8 %collective-permute-start.1 = (bf16[90,16,128]{2,1,0:T(8,128)(2,1)}, bf16[90,16,128]{2,1,0:T(8,128)(2,1)S(1)}, u32[]{:S(2)}, u32[]{:S(2)}) collective-permute-start(bf16[90,16,128]{2,1,0:T(8,128)(2,1)} %get-tuple-element.36), channel_id=1, source_target_pairs={{0,4},{1,5},{2,6},{3,7},{4,8},{5,9},{6,10},{7,11},{8,12},{9,13},{1... | collective-permute-start | bytes 1105928 | tf_op jit(solution)/shard_map/ppermute | solution.py:517
  178.2 31.6 %collective-permute-start.2 = (bf16[90,16,128]{2,1,0:T(8,128)(2,1)}, bf16[90,16,128]{2,1,0:T(8,128)(2,1)S(1)}, u32[]{:S(2)}, u32[]{:S(2)}) collective-permute-start(bf16[90,16,128]{2,1,0:T(8,128)(2,1)} %get-tuple-element.38), channel_id=1, source_target_pairs={{0,12},{1,13},{2,14},{3,15},{4,0},{5,1},{6,2},{7,3},{8,4},{9,5},{1... | collective-permute-start | bytes 1105928 | tf_op jit(solution)/shard_map/ppermute | solution.py:517
  180.3 37.1 %collective-permute-start.3 = (bf16[90,16,128]{2,1,0:T(8,128)(2,1)}, bf16[90,16,128]{2,1,0:T(8,128)(2,1)}, u32[]{:S(2)}, u32[]{:S(2)}) collective-permute-start(bf16[90,16,128]{2,1,0:T(8,128)(2,1)} %get-tuple-element.37), channel_id=1, source_target_pairs={{0,8},{1,9},{2,10},{3,11},{4,12},{5,13},{6,14},{7,15},{8,0},{9,1},... | collective-permute-start | bytes 1105928 | tf_op jit(solution)/shard_map/ppermute | solution.py:517
  209.8 0.8 copy-start.2
  210.5 0.7 copy-start.3
  218.8 9.4 %collective-permute-start.4 = (bf16[90,8,128]{2,1,0:T(8,128)(2,1)S(1)}, bf16[90,8,128]{2,1,0:T(8,128)(2,1)S(1)}, u32[]{:S(2)}, u32[]{:S(2)}) collective-permute-start(bf16[90,8,128]{2,1,0:T(8,128)(2,1)S(1)} %fusion.9), channel_id=1, source_target_pairs={{0,2},{1,3},{2,0},{3,1},{4,6},{5,7},{6,4},{7,5},{8,10},{9,11},{10,... | collective-permute-start | bytes 552968 | tf_op jit(solution)/shard_map/ppermute | solution.py:528
where the time goes:
time: 273 us; the launch traced here: 272 us
  waiting for transfers between devices  111 us (41%)
  starting transfers between devices  44.6 us (16%)
  Pallas kernels  39.4 us (14%)
  blocking collectives  36.6 us (13%)
  local copies, waits for them, and re-layouts  24.4 us (9%)
  other arithmetic  14.6 us (5%)
    all_to_all x5, waiting for transfers between devices, exchange(): return lax.all_to_all(x, axis, split_axis=0, concat_axis=0, tiled=True)  72.5 us
    all_to_all x1, blocking collectives, exchange(): return lax.all_to_all(x, axis, split_axis=0, concat_axis=0, tiled=True)  36.6 us
    all_to_all x5, starting transfers between devices, exchange(): return lax.all_to_all(x, axis, split_axis=0, concat_axis=0, tiled=True)  35 us
    ppermute x3, waiting for transfers between devices, on_device(): got.append(lax.ppermute(sums[step].astype(BF16), 'lon', pairs))  33.9 us
    pallas_call x1, Pallas kernels, legendre_table(): pl.pallas_call(legendre_kernel, out_shape=jax.ShapeDtypeStruct((ORDERS, L...  9.14 us
    optimization_barrier x1, local copies, waits for them, and re-layouts, on_device(): lax.optimization_barrier((rows, forward, legendre))  9.07 us
    pallas_call x1, Pallas kernels, weigh(): pl.pallas_call(weigh_kernel, grid=(steps,), out_shape=(pltpu.HBM(shape, B...  5.91 us
  transfers between devices with their start and end apart: 10, of which 7 were waited for; matrix products, arithmetic and copies ran while one was open for 11% of the time, Pallas kernels for 3%

commit v1 on v0

--- a/solution.py
+++ b/solution.py
@@ -68,14 +68,6 @@
             copy(jnp.minimum(g, steps - 1)).wait()
 
     return arrive
-
-
-def fetch(table, held, ready):
-    parts = range(held.shape[0])
-    copies = [pltpu.make_async_copy(table.at[k], held.at[k], ready.at[k]) for k in parts]
-    for copy in copies:
-        copy.start()
-    return copies
 
 
 def send(made, out, done):
@@ -310,8 +302,12 @@
 
 
 def mix_kernel(x_ref, weights, gathered, out_ref, wide, mixed, rows, made, held, ready, done):
-    copies = fetch(weights, held, ready)
     steps, each = held.shape[:2]
+    copies = [
+        pltpu.make_async_copy(weights.at[k], held.at[k], ready.at[k]) for k in range(steps)
+    ]
+    for copy in copies[:2]:
+        copy.start()
     slabs = LATS * Q
     for slab in range(slabs):
         wide[slab * ODD : slab * ODD + PAD, :] = x_ref[slab * PAD : slab * PAD + PAD, :].astype(
@@ -321,6 +317,8 @@
     sent = []
     for step in range(steps):
         copies[step].wait()
+        if step + 2 < steps:
+            copies[step + 2].start()
         for offset in range(each):
             degree = step * each + offset
             across = pl.ds(degree, slabs, stride=ODD)
@@ -525,11 +523,11 @@
     y = (lax.axis_index("lon") >> 1) & 1
     keep = lax.dynamic_index_in_dim(held, y, 1, keepdims=False)
     give = lax.dynamic_index_in_dim(held, 1 - y, 1, keepdims=False).astype(BF16)
+    row_block, keep, give = lax.optimization_barrier((row_block, keep, give))
+    grid_part = fourier_backward(backward, row_block.reshape(DEVICES * CHUNK, C))
+    grid_part = exchange(grid_part.reshape(LONS, SLOT, PAD, C), "lon")
     got = lax.ppermute(give, "lon", [(k, k ^ 2) for k in range(LONS)])
     weight_grad = keep + got.astype(F32)
-    row_block, weight_grad = lax.optimization_barrier((row_block, weight_grad))
-    grid_part = fourier_backward(backward, row_block.reshape(DEVICES * CHUNK, C))
-    grid_part = exchange(grid_part.reshape(LONS, SLOT, PAD, C), "lon")
     grad_in = grid_part[:USED].reshape(ROWS, PAD, C)[:, :COLS]
     return jnp.swapaxes(grad_in, 1, 2)[None], weight_grad
 

time: 273 us -> 266 us (0.974)
  blocking collectives: 36.6 us -> 0 us
  waiting for transfers between devices: 111 us -> 139 us
  starting transfers between devices: 44.6 us -> 48.1 us
    all_to_all x1 -> x0, blocking collectives: 36.6 us -> none  [exchange(): return lax.all_to_all(x, axis, split_axis=0, concat_axis=0, tiled=True)]
    ppermute x1, waiting for transfers between devices: 4.78 us -> 31 us  [on_device(): got = lax.ppermute(give, 'lon', [(k, k ^ 2) for k in range(LONS)])]
    all_to_all x5 -> x6, starting transfers between devices: 35 us -> 39.7 us  [exchange(): return lax.all_to_all(x, axis, split_axis=0, concat_axis=0, tiled=True)]
    all_to_all x5 -> x6, waiting for transfers between devices: 72.5 us -> 72.5 us  [exchange(): return lax.all_to_all(x, axis, split_axis=0, concat_axis=0, tiled=True)]
  transfers between devices with their start and end apart: 10 -> 11, of which waited for: 7 -> 7; matrix products, arithmetic and copies ran while one was open for 11% -> 11% of each run, Pallas kernels for 3% -> 3%
where the time goes in v1:
time: 266 us; the launch traced here: 265 us
  waiting for transfers between devices  139 us (52%)
  starting transfers between devices  48.1 us (18%)
  Pallas kernels  39.5 us (15%)
  local copies, waits for them, and re-layouts  23 us (9%)
  other arithmetic  14.4 us (5%)
    all_to_all x6, waiting for transfers between devices, exchange(): return lax.all_to_all(x, axis, split_axis=0, concat_axis=0, tiled=True)  72.5 us
    all_to_all x6, starting transfers between devices, exchange(): return lax.all_to_all(x, axis, split_axis=0, concat_axis=0, tiled=True)  39.7 us
    ppermute x3, waiting for transfers between devices, on_device(): got.append(lax.ppermute(sums[step].astype(BF16), 'lon', pairs))  35.4 us
    ppermute x1, waiting for transfers between devices, on_device(): got = lax.ppermute(give, 'lon', [(k, k ^ 2) for k in range(LONS)])  31 us
    pallas_call x1, Pallas kernels, legendre_table(): pl.pallas_call(legendre_kernel, out_shape=jax.ShapeDtypeStruct((ORDERS, L...  9.14 us
    optimization_barrier x1, local copies, waits for them, and re-layouts, on_device(): lax.optimization_barrier((rows, forward, legendre))  9.07 us
    pallas_call x1, Pallas kernels, weigh(): pl.pallas_call(weigh_kernel, grid=(steps,), out_shape=(pltpu.HBM(shape, B...  5.91 us
  transfers between devices with their start and end apart: 11, of which 7 were waited for; matrix products, arithmetic and copies ran while one was open for 11% of the time, Pallas kernels for 3%

profile of v1, /device:TPU:0, one launch (start us, length us, event | category | flops | bytes accessed | tf_op | source)
XLA Modules:
  0.0 264.8 jit_solution(15066135902227199772)
XLA Ops:
  0.6 3.3 %pad.4 = bf16[96,96,128]{2,1,0:T(8,128)(2,1)} pad(bf16[90,90,128]{2,1,0:T(8,128)(2,1)} %bitcast.57, bf16[]{:T(256)} %constant.277.clone.1), padding=0_6x0_6x0_0 | pad | bytes 4432898 | tf_op jit(solution)/shard_map/jit(_pad)/pad | solution.py:491
  3.9 8.2 %all-to-all-start = ((bf16[16,6,96,128]{3,2,1,0:T(8,128)(2,1)}), bf16[16,6,96,128]{3,2,1,0:T(8,128)(2,1)S(1)}, u32[]{:S(2)}, u32[]{:S(2)}) async-start(bf16[16,6,96,128]{3,2,1,0:T(8,128)(2,1)} %bitcast.50), calls=%async_computation | async-start | bytes 4718592 | tf_op jit(solution)/shard_map/all_to_all | solution.py:481
  12.1 0.1 subtract_multiply_fusion
  12.2 0.1 mul.419
  12.3 0.1 sub.152
  12.3 0.1 fusion.10
  12.4 0.1 gt.23
  12.6 0.1 div.175
  12.6 0.1 mul.421
  12.7 0.1 reshape.688.start
  12.8 0.7 fusion.76.seed
  13.5 0.1 fusion.75.sine_ref
  13.6 0.1 sqrt_select_fusion.2
  13.7 9.1 %legendre.1.table = bf16[5,768,768]{2,1,0:T(8,128)(2,1)S(1)} custom-call(f32[3600]{0:T(1024)S(1)} %get-tuple-element.43.up, f32[3600]{0:T(1024)S(1)} %get-tuple-element.42.back, f32[3600]{0:T(1024)S(1)} %reshape.688.start, f32[5]{0:T(128)S(1)} %fusion.76.seed, f32[5]{0:T(128)S(1)} %get-tuple-element.36.order, f32[8,128]{1,0:T(8,128)S(1)} %get-tuple-element.51.x_ref, ...), custom_call_target="tpu_custom_call" | custom-call | tf_op jit(solution)/shard_map/legendre/pallas_call | solution.py:216
  22.8 0.0 copy-start
  22.8 2.5 copy-done
  25.4 0.1 fusion.48
  25.5 4.3 %multiply_convert_fusion.1.table = bf16[2,640,768]{2,1,0:T(8,128)(2,1)} fusion(f32[768]{0:T(1024)S(1)} %fusion.69, f32[2,640]{1,0:T(2,128)S(1)} %fusion.46, f32[2,640]{1,0:T(2,128)S(1)} %fusion.48, f32[768]{0:T(1024)S(1)} %fusion.54), kind=kLoop, calls=%fused_computation.7 | loop fusion | flops 24576000 | bytes 1982464 | tf_op jit(solution)/shard_map/convert_element_type | solution.py:117
  29.8 14.3 %all-to-all-done.x_ref = bf16[16,6,96,128]{3,2,1,0:T(8,128)(2,1)S(1)} async-done(((bf16[16,6,96,128]{3,2,1,0:T(8,128)(2,1)}), bf16[16,6,96,128]{3,2,1,0:T(8,128)(2,1)S(1)}, u32[]{:S(2)}, u32[]{:S(2)}) %all-to-all-start) | async-done | bytes 2359328 | tf_op jit(solution)/shard_map/all_to_all | solution.py:481
  44.1 4.3 %fourier_forward.1 = bf16[4,2,960,128]{3,2,1,0:T(8,128)(2,1)} custom-call(bf16[2,640,768]{2,1,0:T(8,128)(2,1)} %multiply_convert_fusion.1.table, bf16[16,6,96,128]{3,2,1,0:T(8,128)(2,1)S(1)} %all-to-all-done.x_ref), custom_call_target="tpu_custom_call" | custom-call | tf_op jit(solution)/shard_map/fourier_forward/pallas_call | solution.py:260
  48.5 6.2 %all-to-all-start.1 = ((bf16[128,30,2,128]{3,2,1,0:T(2,128)(2,1)}), bf16[128,30,2,128]{3,2,1,0:T(2,128)(2,1)S(1)}, u32[]{:S(2)}, u32[]{:S(2)}) async-start(bf16[128,30,2,128]{3,2,1,0:T(2,128)(2,1)} %bitcast.54), calls=%async_computation.1 | async-start | bytes 3932160 | tf_op jit(solution)/shard_map/all_to_all | solution.py:481
  54.7 4.0 %copy.7 = bf16[5,8,90,2,128]{4,3,0,1,2:T(2,128)(2,1)} copy(bf16[5,8,90,2,128]{4,3,2,1,0:T(2,128)(2,1)} %bitcast.59) | data formatting | bytes 3686400 | tf_op jit(solution)/shard_map/reshape | solution.py:500
  58.7 9.1 %copy.6 = bf16[5,768,768]{1,2,0:T(8,128)(2,1)} copy(bf16[5,768,768]{2,1,0:T(8,128)(2,1)} %copy-done) | data formatting | bytes 11796480 | tf_op jit(solution)/shard_map/optimization_barrier | solution.py:495
  67.8 14.4 %all-to-all-done.1 = bf16[128,30,2,128]{3,2,1,0:T(2,128)(2,1)S(1)} async-done(((bf16[128,30,2,128]{3,2,1,0:T(2,128)(2,1)}), bf16[128,30,2,128]{3,2,1,0:T(2,128)(2,1)S(1)}, u32[]{:S(2)}, u32[]{:S(2)}) %all-to-all-start.1) | async-done | bytes 1966112 | tf_op jit(solution)/shard_map/all_to_all | solution.py:481
  82.1 5.1 %analyse.1 = bf16[8,10,96,128]{3,2,1,0:T(8,128)(2,1)} custom-call(bf16[5,768,768]{2,1,0:T(8,128)(2,1)} %copy-done, bf16[7680,128]{1,0:T(8,128)(2,1)S(1)} %bitcast.45), custom_call_target="tpu_custom_call" | custom-call | tf_op jit(solution)/shard_map/analyse/pallas_call | solution.py:292
  87.3 3.8 %all-to-all-start.2 = ((bf16[8,10,96,128]{3,2,1,0:T(8,128)(2,1)}), bf16[8,10,96,128]{3,2,1,0:T(8,128)(2,1)S(1)}, u32[]{:S(2)}, u32[]{:S(2)}) async-start(bf16[8,10,96,128]{3,2,1,0:T(8,128)(2,1)} %analyse.1), calls=%async_computation.2 | async-start | bytes 3932160 | tf_op jit(solution)/shard_map/all_to_all | solution.py:481
  91.1 0.1 pad_add_fusion.place
  91.2 4.6 %multiply_convert_fusion = bf16[768,1280]{1,0:T(8,128)(2,1)} fusion(f32[768]{0:T(1024)S(1)} %fusion.69, f32[1280]{0:T(1024)S(1)} %fusion.25, f32[1280]{0:T(1024)S(1)} %fusion.20, f32[768]{0:T(1024)S(1)} %fusion.54), kind=kLoop, calls=%fused_computation | loop fusion | flops 24576000 | bytes 1982464 | tf_op jit(solution)/shard_map/convert_element_type | solution.py:120
  95.8 21.8 %all-to-all-done.2 = bf16[8,10,96,128]{3,2,1,0:T(8,128)(2,1)S(1)} async-done(((bf16[8,10,96,128]{3,2,1,0:T(8,128)(2,1)}), bf16[8,10,96,128]{3,2,1,0:T(8,128)(2,1)S(1)}, u32[]{:S(2)}, u32[]{:S(2)}) %all-to-all-start.2) | async-done | bytes 1966112 | tf_op jit(solution)/shard_map/all_to_all | solution.py:481
  117.6 5.2 %mix.1 = (bf16[90,80,128]{2,1,0:T(8,128)(2,1)}, bf16[7680,128]{1,0:T(8,128)(2,1)}) custom-call(bf16[7680,128]{1,0:T(8,128)(2,1)S(1)} %bitcast.47, bf16[5,18,128,128]{3,2,1,0:T(8,128)(2,1)} %bitcast.56), custom_call_target="tpu_custom_call" | custom-call | tf_op jit(solution)/shard_map/mix/pallas_call | solution.py:347
  122.8 5.9 %weigh.1 = (bf16[4,90,16,128]{3,2,1,0:T(8,128)(2,1)}, bf16[4,90,16,128]{3,2,1,0:T(8,128)(2,1)}) custom-call(s32[2]{0:T(128)S(1)} %pad_add_fusion.place, bf16[90,80,128]{2,1,0:T(8,128)(2,1)} %bitcast.55, bf16[90,80,128]{2,1,0:T(8,128)(2,1)} %get-tuple-element.28.gathered), custom_call_target="tpu_custom_call" | custom-call | tf_op jit(solution)/shard_map/weigh/pallas_call | solution.py:387
  128.7 0.0 collective-permute-start
  128.7 8.5 %all-to-all-start.3 = ((bf16[8,10,96,128]{3,2,1,0:T(8,128)(2,1)}), bf16[8,10,96,128]{3,2,1,0:T(8,128)(2,1)S(1)}, u32[]{:S(2)}, u32[]{:S(2)}) async-start(bf16[8,10,96,128]{3,2,1,0:T(8,128)(2,1)} %bitcast.58), calls=%async_computation.3 | async-start | bytes 3932160 | tf_op jit(solution)/shard_map/all_to_all | solution.py:481
  137.3 0.0 collective-permute-done
  137.3 0.0 copy-start.1
  137.3 1.2 copy-done.1
  138.5 3.0 %fusion.6 = (bf16[90,16,128]{2,1,0:T(8,128)(2,1)}, bf16[90,16,128]{2,1,0:T(8,128)(2,1)}, bf16[90,16,128]{2,1,0:T(8,128)(2,1)}, f32[90,16,128]{2,1,0:T(8,128)S(1)}) fusion(bf16[4,90,16,128]{3,2,1,0:T(8,128)(2,1)} %copy-done.1, bf16[4,90,16,128]{3,2,1,0:T(8,128)(2,1)} %get-tuple-element.29), kind=kLoop, calls=%fused_computation.20 | loop fusion | flops 2764800 | bytes 4792320 | tf_op jit(solution)/shard_map/convert_element_type | solution.py:515
  141.5 22.0 %all-to-all-done.3.x_ref = bf16[8,10,96,128]{3,2,1,0:T(8,128)(2,1)S(1)} async-done(((bf16[8,10,96,128]{3,2,1,0:T(8,128)(2,1)}), bf16[8,10,96,128]{3,2,1,0:T(8,128)(2,1)S(1)}, u32[]{:S(2)}, u32[]{:S(2)}) %all-to-all-start.3) | async-done | bytes 1966112 | tf_op jit(solution)/shard_map/all_to_all | solution.py:481
  163.5 5.3 %synthesise.1 = bf16[7680,128]{1,0:T(8,128)(2,1)} custom-call(bf16[5,768,768]{2,1,0:T(8,128)(2,1)} %bitcast.48, bf16[8,10,96,128]{3,2,1,0:T(8,128)(2,1)S(1)} %all-to-all-done.3.x_ref), custom_call_target="tpu_custom_call" | custom-call | tf_op jit(solution)/shard_map/synthesise/pallas_call | solution.py:418
  168.7 8.4 %all-to-all-start.4 = ((bf16[128,30,2,128]{3,2,1,0:T(2,128)(2,1)}), bf16[128,30,2,128]{3,2,1,0:T(2,128)(2,1)S(1)}, u32[]{:S(2)}, u32[]{:S(2)}) async-start(bf16[128,30,2,128]{3,2,1,0:T(2,128)(2,1)} %bitcast.52), calls=%async_computation.4 | async-start | bytes 3932160 | tf_op jit(solution)/shard_map/all_to_all | solution.py:481
  177.1 1.1 collective-permute-start.1
  178.2 2.2 collective-permute-start.2
  180.4 1.6 collective-permute-start.3
  182.1 27.8 %collective-permute-done.1 = bf16[90,16,128]{2,1,0:T(8,128)(2,1)S(1)} collective-permute-done((bf16[90,16,128]{2,1,0:T(8,128)(2,1)}, bf16[90,16,128]{2,1,0:T(8,128)(2,1)S(1)}, u32[]{:S(2)}, u32[]{:S(2)}) %collective-permute-start.1) | collective-permute-done | bytes 368672 | tf_op jit(solution)/shard_map/ppermute | solution.py:515
  209.9 0.0 collective-permute-done.2
  209.9 7.6 %collective-permute-done.3 = bf16[90,16,128]{2,1,0:T(8,128)(2,1)} collective-permute-done((bf16[90,16,128]{2,1,0:T(8,128)(2,1)}, bf16[90,16,128]{2,1,0:T(8,128)(2,1)}, u32[]{:S(2)}, u32[]{:S(2)}) %collective-permute-start.3) | collective-permute-done | bytes 368672 | tf_op jit(solution)/shard_map/ppermute | solution.py:515
  217.5 1.2 add_bitcast_fusion
  218.7 0.0 all-to-all-done.4
  218.8 4.5 %fourier_backward.1 = bf16[2,8,6,96,128]{4,3,2,1,0:T(8,128)(2,1)} custom-call(bf16[2,384,1280]{2,1,0:T(8,128)(2,1)} %bitcast.53, bf16[7680,128]{1,0:T(8,128)(2,1)S(1)} %bitcast.46), custom_call_target="tpu_custom_call" | custom-call | tf_op jit(solution)/shard_map/fourier_backward/pallas_call | solution.py:464
  223.2 4.7 %all-to-all-start.5 = ((bf16[16,6,96,128]{3,2,1,0:T(8,128)(2,1)}), bf16[16,6,96,128]{3,2,1,0:T(8,128)(2,1)S(1)}, u32[]{:S(2)}, u32[]{:S(2)}) async-start(bf16[16,6,96,128]{3,2,1,0:T(8,128)(2,1)} %bitcast.49), calls=%async_computation.5 | async-start | bytes 4718592 | tf_op jit(solution)/shard_map/all_to_all | solution.py:481
  227.9 3.4 %collective-permute-start.4 = (bf16[90,8,128]{2,1,0:T(8,128)(2,1)S(1)}, bf16[90,8,128]{2,1,0:T(8,128)(2,1)S(1)}, u32[]{:S(2)}, u32[]{:S(2)}) collective-permute-start(bf16[90,8,128]{2,1,0:T(8,128)(2,1)S(1)} %fusion.9), channel_id=1, source_target_pairs={{0,2},{1,3},{2,0},{3,1},{4,6},{5,7},{6,4},{7,5},{8,10},{9,11},{10,... | collective-permute-start | bytes 552968 | tf_op jit(solution)/shard_map/ppermute | solution.py:529
  231.4 31.0 %collective-permute-done.4 = bf16[90,8,128]{2,1,0:T(8,128)(2,1)S(1)} collective-permute-done((bf16[90,8,128]{2,1,0:T(8,128)(2,1)S(1)}, bf16[90,8,128]{2,1,0:T(8,128)(2,1)S(1)}, u32[]{:S(2)}, u32[]{:S(2)}) %collective-permute-start.4) | collective-permute-done | bytes 184352 | tf_op jit(solution)/shard_map/ppermute | solution.py:529
  262.3 0.8 convert_add_fusion
  263.1 0.0 all-to-all-done.5
  263.1 0.1 slice.44
  263.3 1.5 slice_bitcast_fusion
  (16 shorter events, 0.2 us)
Async XLA Ops:
  3.9 40.2 %all-to-all-start = ((bf16[16,6,96,128]{3,2,1,0:T(8,128)(2,1)}), bf16[16,6,96,128]{3,2,1,0:T(8,128)(2,1)S(1)}, u32[]{:S(2)}, u32[]{:S(2)}) async-start(bf16[16,6,96,128]{3,2,1,0:T(8,128)(2,1)} %bitcast.50), calls=%async_computation | async-start | bytes 4718592 | tf_op jit(solution)/shard_map/all_to_all | solution.py:481
  22.8 2.5 copy-start
  48.5 33.7 %all-to-all-start.1 = ((bf16[128,30,2,128]{3,2,1,0:T(2,128)(2,1)}), bf16[128,30,2,128]{3,2,1,0:T(2,128)(2,1)S(1)}, u32[]{:S(2)}, u32[]{:S(2)}) async-start(bf16[128,30,2,128]{3,2,1,0:T(2,128)(2,1)} %bitcast.54), calls=%async_computation.1 | async-start | bytes 3932160 | tf_op jit(solution)/shard_map/all_to_all | solution.py:481
  87.3 30.3 %all-to-all-start.2 = ((bf16[8,10,96,128]{3,2,1,0:T(8,128)(2,1)}), bf16[8,10,96,128]{3,2,1,0:T(8,128)(2,1)S(1)}, u32[]{:S(2)}, u32[]{:S(2)}) async-start(bf16[8,10,96,128]{3,2,1,0:T(8,128)(2,1)} %analyse.1), calls=%async_computation.2 | async-start | bytes 3932160 | tf_op jit(solution)/shard_map/all_to_all | solution.py:481
  128.7 8.5 %collective-permute-start = (bf16[4,90,16,128]{3,2,1,0:T(8,128)(2,1)}, bf16[4,90,16,128]{3,2,1,0:T(8,128)(2,1)S(1)}, u32[]{:S(2)}, u32[]{:S(2)}) collective-permute-start(bf16[4,90,16,128]{3,2,1,0:T(8,128)(2,1)} %get-tuple-element.30), channel_id=1, source_target_pairs={{0,1},{1,0},{2,3},{3,2},{4,5},{5,4},{6,7},{7,6},{8,9},{9,8},{10,11... | collective-permute-start | bytes 4423688 | tf_op jit(solution)/shard_map/ppermute | solution.py:510
  128.7 34.7 %all-to-all-start.3 = ((bf16[8,10,96,128]{3,2,1,0:T(8,128)(2,1)}), bf16[8,10,96,128]{3,2,1,0:T(8,128)(2,1)S(1)}, u32[]{:S(2)}, u32[]{:S(2)}) async-start(bf16[8,10,96,128]{3,2,1,0:T(8,128)(2,1)} %bitcast.58), calls=%async_computation.3 | async-start | bytes 3932160 | tf_op jit(solution)/shard_map/all_to_all | solution.py:481
  137.3 1.2 copy-start.1
  168.7 50.0 %all-to-all-start.4 = ((bf16[128,30,2,128]{3,2,1,0:T(2,128)(2,1)}), bf16[128,30,2,128]{3,2,1,0:T(2,128)(2,1)S(1)}, u32[]{:S(2)}, u32[]{:S(2)}) async-start(bf16[128,30,2,128]{3,2,1,0:T(2,128)(2,1)} %bitcast.52), calls=%async_computation.4 | async-start | bytes 3932160 | tf_op jit(solution)/shard_map/all_to_all | solution.py:481
  177.1 32.8 %collective-permute-start.1 = (bf16[90,16,128]{2,1,0:T(8,128)(2,1)}, bf16[90,16,128]{2,1,0:T(8,128)(2,1)S(1)}, u32[]{:S(2)}, u32[]{:S(2)}) collective-permute-start(bf16[90,16,128]{2,1,0:T(8,128)(2,1)} %get-tuple-element.38), channel_id=1, source_target_pairs={{0,4},{1,5},{2,6},{3,7},{4,8},{5,9},{6,10},{7,11},{8,12},{9,13},{1... | collective-permute-start | bytes 1105928 | tf_op jit(solution)/shard_map/ppermute | solution.py:515
  178.2 31.6 %collective-permute-start.2 = (bf16[90,16,128]{2,1,0:T(8,128)(2,1)}, bf16[90,16,128]{2,1,0:T(8,128)(2,1)S(1)}, u32[]{:S(2)}, u32[]{:S(2)}) collective-permute-start(bf16[90,16,128]{2,1,0:T(8,128)(2,1)} %get-tuple-element.40), channel_id=1, source_target_pairs={{0,12},{1,13},{2,14},{3,15},{4,0},{5,1},{6,2},{7,3},{8,4},{9,5},{1... | collective-permute-start | bytes 1105928 | tf_op jit(solution)/shard_map/ppermute | solution.py:515
  180.4 37.1 %collective-permute-start.3 = (bf16[90,16,128]{2,1,0:T(8,128)(2,1)}, bf16[90,16,128]{2,1,0:T(8,128)(2,1)}, u32[]{:S(2)}, u32[]{:S(2)}) collective-permute-start(bf16[90,16,128]{2,1,0:T(8,128)(2,1)} %get-tuple-element.39), channel_id=1, source_target_pairs={{0,8},{1,9},{2,10},{3,11},{4,12},{5,13},{6,14},{7,15},{8,0},{9,1},... | collective-permute-start | bytes 1105928 | tf_op jit(solution)/shard_map/ppermute | solution.py:515
  223.2 39.9 %all-to-all-start.5 = ((bf16[16,6,96,128]{3,2,1,0:T(8,128)(2,1)}), bf16[16,6,96,128]{3,2,1,0:T(8,128)(2,1)S(1)}, u32[]{:S(2)}, u32[]{:S(2)}) async-start(bf16[16,6,96,128]{3,2,1,0:T(8,128)(2,1)} %bitcast.49), calls=%async_computation.5 | async-start | bytes 4718592 | tf_op jit(solution)/shard_map/all_to_all | solution.py:481
  227.9 34.4 %collective-permute-start.4 = (bf16[90,8,128]{2,1,0:T(8,128)(2,1)S(1)}, bf16[90,8,128]{2,1,0:T(8,128)(2,1)S(1)}, u32[]{:S(2)}, u32[]{:S(2)}) collective-permute-start(bf16[90,8,128]{2,1,0:T(8,128)(2,1)S(1)} %fusion.9), channel_id=1, source_target_pairs={{0,2},{1,3},{2,0},{3,1},{4,6},{5,7},{6,4},{7,5},{8,10},{9,11},{10,... | collective-permute-start | bytes 552968 | tf_op jit(solution)/shard_map/ppermute | solution.py:529
